TPU v7x, 256 devices: a whole 4x4x8 slice. The times are simulated.
256 devices in a mesh: rep: 2 (over core), seq: 16 (over z, y_hi), head: 8 (over y_lo, x).
Axes of the slice: x: 4, y: 4 (y_hi: 2, y_lo: 2; y = y_hi * 2 + y_lo), z: 8, core: 2. Of those that a mesh axis runs over, the one named last changes fastest.
Arguments:
- query_latent: bfloat16 [2, 2048, 1536], P('rep', 'seq'), may hold values from -72 to 72
- kv_latent: bfloat16 [2, 2048, 576], P('rep', 'seq'), may hold values from -72 to 72
- query_up: bfloat16 [1536, 12288], P(None, 'head'), may hold values from -0.15625 to 0.15625
- kv_up: bfloat16 [512, 16384], P(None, 'head'), may hold values from -0.25 to 0.25
- out_grad: bfloat16 [2, 2048, 8192], P('rep', 'seq', 'head'), may hold values from -6 to 6
- positions: int32 [2, 2048], P('rep'), may hold values from 0 to 1535, as said below
Outputs:
- query_grad: bfloat16 [2, 2048, 1536], P('rep', 'seq')
- latent_grad: bfloat16 [2, 2048, 576], P('rep', ('seq', 'head'))
- query_up_grad: bfloat16 [1536, 12288], P(('rep', 'seq'), 'head')
Inputs may be any that keep to these rules, and one draw needn't show every extreme that they name: In each window, positions count tokens from the start of their document, rising by one a token and restarting at 0 where a document begins; a window's first token has position 0; the first document is exactly 1536 tokens long and no document is longer.
All inputs are finite; a program needn't handle non-finite values.
Results may differ from a plain program's by a relative error of at most 0.013.
The roundings to bfloat16 on the way count: a program that leaves them out, or rounds other values in their place, can miss the bound.
Values may be sent and summed in bfloat16 or wider, within the bound.
A program may use at most 128 MiB of HBM per device.

v0:
```python
import jax
import jax.numpy as jnp
from jax import lax
from jax.sharding import PartitionSpec as P

QL = 1536
KVL = 512
ROPE = 64
NOPE = 128
VD = 128


def rope_tables(positions):
    half_rope = ROPE // 2
    rotation_rates = 10000.0 ** (-jnp.arange(half_rope, dtype=jnp.float32) / half_rope)
    angles = positions.astype(jnp.float32)[:, None] * rotation_rates[None, :]
    return (jnp.cos(angles), jnp.sin(angles))


def rotate(vector, cosine, sine_table):
    half_rope = ROPE // 2
    front_half = vector[..., :half_rope]
    back_half = vector[..., half_rope:]
    return jnp.concatenate(
        [
            front_half * cosine - back_half * sine_table,
            front_half * sine_table + back_half * cosine,
        ],
        -1,
    )


def unrotate(vector, cosine, sine_table):
    half_rope = ROPE // 2
    front_half = vector[..., :half_rope]
    back_half = vector[..., half_rope:]
    return jnp.concatenate(
        [
            front_half * cosine + back_half * sine_table,
            back_half * cosine - front_half * sine_table,
        ],
        -1,
    )


def shards(query_latent, kv_latent, query_up, kv_up, out_grad, positions):
    tok_dev = query_latent.shape[1]
    heads_dev = query_up.shape[1] // (NOPE + ROPE)
    tokens = tok_dev * lax.axis_size("seq")
    first_row = lax.axis_index("seq") * tok_dev
    local_latent = query_latent[0]
    all_positions = positions[0]
    local_positions = lax.dynamic_slice_in_dim(all_positions, first_row, tok_dev)
    token_index = jnp.arange(tokens, dtype=jnp.int32)
    query_index = first_row + jnp.arange(tok_dev, dtype=jnp.int32)
    visible = (token_index[None, :] <= query_index[:, None]) & (
        local_positions[:, None] - all_positions[None, :]
        == query_index[:, None] - token_index[None, :]
    )
    cosine, sine_table = rope_tables(local_positions)
    softmax_scale = (NOPE + ROPE) ** (-0.5)
    query_weight = query_up.reshape(QL, heads_dev, NOPE + ROPE)
    kv_weight = kv_up.reshape(KVL, heads_dev, NOPE + VD)
    grad_heads = out_grad[0].reshape(tok_dev, heads_dev, VD).transpose(1, 0, 2)
    shard_rows = lax.all_gather(kv_latent[0], "seq", axis=0, tiled=True)
    projected = jnp.einsum(
        "tc,chd->htd", shard_rows[:, :KVL], kv_weight, preferred_element_type=jnp.float32
    )
    key_rope = jnp.broadcast_to(
        shard_rows[None, :, KVL:].astype(jnp.float32), (heads_dev, shard_rows.shape[0], ROPE)
    )
    key_value = jnp.concatenate(
        [projected[..., :NOPE], key_rope, projected[..., NOPE:]], -1
    ).astype(jnp.bfloat16)
    key_rows = key_value[..., : NOPE + ROPE]
    values = key_value[..., NOPE + ROPE :]
    projected_q = jnp.einsum(
        "tq,qhd->htd", local_latent, query_weight, preferred_element_type=jnp.float32
    )
    queries = jnp.concatenate(
        [projected_q[..., :NOPE], rotate(projected_q[..., NOPE:], cosine, sine_table)], -1
    ).astype(jnp.bfloat16)
    scores = (
        jnp.einsum("hqd,hkd->hqk", queries, key_rows, preferred_element_type=jnp.float32)
        * softmax_scale
    )
    scores = jnp.where(visible[None], scores, -jnp.inf)
    row_max = jnp.max(scores, 2, keepdims=True)
    exponent = jnp.exp(scores - row_max)
    attention = exponent / jnp.sum(exponent, 2, keepdims=True)
    prob_grad = jnp.einsum("hqd,hkd->hqk", grad_heads, values, preferred_element_type=jnp.float32)
    row_inner = jnp.sum(attention * prob_grad, 2, keepdims=True)
    score_grad = (attention * (prob_grad - row_inner) * softmax_scale).astype(jnp.bfloat16)
    attention_low = attention.astype(jnp.bfloat16)
    value_grad = jnp.einsum(
        "hqk,hqd->hkd", attention_low, grad_heads, preferred_element_type=jnp.float32
    ).astype(jnp.bfloat16)
    query_rows_grad = jnp.einsum(
        "hqk,hkd->hqd", score_grad, key_rows, preferred_element_type=jnp.float32
    )
    key_grad = jnp.einsum(
        "hqk,hqd->hkd", score_grad, queries, preferred_element_type=jnp.float32
    ).astype(jnp.bfloat16)
    head_query_grad = jnp.concatenate(
        [query_rows_grad[..., :NOPE], unrotate(query_rows_grad[..., NOPE:], cosine, sine_table)], -1
    ).astype(jnp.bfloat16)
    query_term = jnp.einsum(
        "htd,qhd->tq", head_query_grad, query_weight, preferred_element_type=jnp.float32
    )
    query_grad = lax.psum(query_term, "head").astype(jnp.bfloat16)[None]
    weight_term = jnp.einsum(
        "tq,htd->qhd", local_latent, head_query_grad, preferred_element_type=jnp.float32
    )
    weight_term = weight_term.reshape(QL, heads_dev * (NOPE + ROPE))
    kv_rows_grad = jnp.concatenate([key_grad[..., :NOPE], value_grad], -1)
    rope_grad = key_grad[..., NOPE:]
    latent_part = jnp.einsum(
        "htd,chd->tc", kv_rows_grad, kv_weight, preferred_element_type=jnp.float32
    )
    latent_grad = lax.psum_scatter(
        jnp.concatenate([latent_part, jnp.sum(rope_grad.astype(jnp.float32), 0)], -1),
        ("seq", "head"),
        scatter_dimension=0,
        tiled=True,
    )
    weight_grad = lax.psum_scatter(weight_term, ("rep", "seq"), scatter_dimension=0, tiled=True)
    return (query_grad, latent_grad.astype(jnp.bfloat16)[None], weight_grad.astype(jnp.bfloat16))


def solution(mesh):
    return jax.shard_map(
        shards,
        mesh=mesh,
        in_specs=(
            P("rep", "seq", None),
            P("rep", "seq", None),
            P(None, "head"),
            P(None, "head"),
            P("rep", "seq", "head"),
            P("rep", None),
        ),
        out_specs=(
            P("rep", "seq", None),
            P("rep", ("seq", "head"), None),
            P(("rep", "seq"), "head"),
        ),
        check_vma=False,
    )
```

profile of v0, /device:TPU:2, one launch (start us, length us, event | category | flops | bytes accessed | tf_op | source)
XLA Modules:
  0.0 1039.1 jit_solution(3629060452253005470)
XLA Ops:
  7.2 1.7 copy.33
  10.2 6.7 copy.32
  16.9 3.7 convolution_bitcast_fusion.1
  20.9 1.2 fusion.30
  22.1 80.6 %all-gather.3.cloned.1.call-done = bf16[1,2048,576]{2,1,0:T(8,128)(2,1)} async-done(((bf16[1,128,576]{2,1,0:T(8,128)(2,1)}), bf16[1,2048,576]{2,1,0:T(8,128)(2,1)}) %all-gather.3.cloned.1.call-update) | async-done | bytes 2359312 | tf_op jit(solution)/shard_map/all_gather | solution.py:65
  103.9 6.8 convert_bitcast_fusion
  111.2 4.5 fusion.12
  116.0 2.0 fusion.11
  118.1 5.7 fusion.47
  123.7 6.7 fusion.19
  130.4 15.9 %convolution_convert_fusion = bf16[8,2048,192]{1,2,0:T(8,128)(2,1)} fusion(f32[8,2048,128]{1,2,0:T(8,128)} %fusion.12, bf16[8,128,32]{1,2,0:T(8,128)(2,1)S(1)} %get-tuple-element.17, bf16[8,128,32]{1,2,0:T(8,128)(2,1)S(1)} %get-tuple-element.16, bf16[8,128,128]{1,2,0:T(8,128)(2,1)S(1)} %slice.89, f32[8,128,2048]{2,1,0:T(8,128)} %get-tuple-element.21, ...), kind=kOutput, calls=%fused_computation.19 | convolution fusion | flops 824314880 | bytes 23465984 | tf_op jit(solution)/shard_map/hqk,hqd->hkd/dot_general | solution.py:101
  146.3 2.1 convert_reduce_fusion
  149.8 1.2 copy-done.5
  151.0 4.5 fusion.23
  155.5 2.7 pad_maximum_fusion.3
  158.1 5.8 copy.49
  164.0 14.5 %fusion.10 = f32[8,128,192]{1,2,0:T(8,128)S(1)} fusion(bf16[8,2048,64]{1,2,0:T(8,128)(2,1)S(1)} %broadcast_in_dim.15, bf16[8,2048,128]{1,2,0:T(8,128)(2,1)} %copy-done.1, f32[8,2048,128]{1,2,0:T(8,128)} %fusion.12, f32[8,128,2048]{2,1,0:T(8,128)} %get-tuple-element.21, f32[8,128]{1,0:T(8,128)S(1)} %get-tuple-element.20), kind=kOutput, calls=%fused_computation.16 | convolution fusion | flops 832572416 | bytes 23859200 | tf_op jit(solution)/shard_map/hqk,hkd->hqd/dot_general | solution.py:98
  178.7 5.0 fusion.31
  183.7 9.6 copy.42
  193.4 3.2 convolution_bitcast_fusion
  196.5 38.2 %all-reduce.1 = bf16[128,1536]{1,0:T(8,128)(2,1)} all-reduce(f32[128,1536]{1,0:T(8,128)S(1)} %convolution_bitcast_fusion), channel_id=1, replica_groups=mesh['rep'=2,'seq'=16,'head'=8] {'head'}, use_global_device_ids=true, to_apply=%region_3.4 | all-reduce | flops 196608 | bytes 1179648 | tf_op jit(solution)/shard_map/psum | solution.py:110
  234.8 631.5 %reduce-scatter.7.cloned.1.call-done = f32[16,576]{1,0:T(8,128)} async-done(((f32[2048,576]{1,0:T(8,128)}), f32[16,576]{1,0:T(8,128)}) %reduce-scatter.7.cloned.1.call-update) | async-done | bytes 36880
  867.9 163.1 %reduce-scatter.5.cloned.1.call-done = f32[48,1536]{1,0:T(8,128)} async-done(((f32[1536,1536]{1,0:T(8,128)}), f32[48,1536]{1,0:T(8,128)}) %reduce-scatter.5.cloned.1.call-update) | async-done | bytes 294928 | tf_op jit(solution)/shard_map/reduce_scatter | solution.py:126
  1030.9 1.6 convert_element_type.44
  (34 shorter events, 6.6 us)
Async XLA Ops:
  7.2 9.7 copy-start
  7.2 95.4 %all-gather.3.cloned.1.call-start = ((), (), s32[]{:S(2)}) async-start(), calls=%async_computation.3 | async-start | bytes 2785280 | tf_op jit(solution)/shard_map/all_gather | solution.py:65
  9.0 857.2 %reduce-scatter.7.cloned.1.call-start = ((), (), s32[]{:S(2)}) async-start(), calls=%async_computation.4 | async-start | bytes 5283840
  10.2 10.5 %copy-start.3 = (s32[1,2048]{1,0:T(1,128)S(1)}, s32[1,2048]{1,0:T(1,128)}, u32[]{:S(2)}) copy-start(s32[1,2048]{1,0:T(1,128)} %param.11) | copy-start | bytes 24580
  111.2 4.8 copy-start.1
  116.0 2.0 copy-start.2
  146.3 2.8 slice-start
  146.3 3.5 copy-start.4
  146.3 4.7 copy-start.5
  164.0 867.0 %reduce-scatter.5.cloned.1.call-start = ((), (), s32[]{:S(2)}) async-start(), calls=%async_computation.2 | async-start | bytes 9732096 | tf_op jit(solution)/shard_map/reduce_scatter | solution.py:126
Sparse Core Ops, SparseCore 0:
  10.6 92.0 all-gather.2
  164.1 702.0 reduce-scatter.6
  870.7 160.2 reduce-scatter.4
where the time goes:
time: 1040 us
  waiting for transfers between devices  875 us (84%)
  matrix products  66.8 us (6%)
  blocking collectives  38.2 us (4%)
  local copies, waits for them, and re-layouts  31.3 us (3%)
  between operations  14 us (1%)
  other arithmetic  13.5 us (1%)
    unnamed x4, waiting for transfers between devices  632 us
    reduce_scatter x1, waiting for transfers between devices, shards(): lax.psum_scatter(weight_term, ('rep', 'seq'), scatter_dimension=0, tiled=...  163 us
    all_gather x1, waiting for transfers between devices, shards(): shard_rows = lax.all_gather(kv_latent[0], 'seq', axis=0, tiled=True)  80.6 us
    psum x1, blocking collectives, shards(): query_grad = lax.psum(query_term, 'head').astype(jnp.bfloat16)[None]  38.2 us
  transfers between devices with their start and end apart: 3, of which 3 were waited for; matrix products, arithmetic and copies ran while one was open for 5% of the time, Pallas kernels for 0%

commit v1 on v0

--- a/solution.py
+++ b/solution.py
@@ -107,7 +107,9 @@
     query_term = jnp.einsum(
         "htd,qhd->tq", head_query_grad, query_weight, preferred_element_type=jnp.float32
     )
-    query_grad = lax.psum(query_term, "head").astype(jnp.bfloat16)[None]
+    query_grad = jnp.sum(lax.all_gather(query_term, axis_name="head"), axis=0).astype(jnp.bfloat16)[
+        None
+    ]
     weight_term = jnp.einsum(
         "tq,htd->qhd", local_latent, head_query_grad, preferred_element_type=jnp.float32
     )

time: 1040 us -> 1110 us (1.067)
  waiting for transfers between devices: 875 us -> 982 us
  blocking collectives: 38.2 us -> 0 us
    all_gather x0 -> x1, waiting for transfers between devices: none -> 71.6 us  [shards(): lax.all_gather(query_term, axis_name='head')]
    psum x1 -> x0, blocking collectives: 38.2 us -> none  [shards(): query_grad = lax.psum(query_term, 'head').astype(jnp.bfloat16)[None]]
    unnamed x4 -> x5, waiting for transfers between devices: 632 us -> 669 us
  transfers between devices with their start and end apart: 3 -> 4, of which waited for: 3 -> 4; matrix products, arithmetic and copies ran while one was open for 5% -> 5% of each run, Pallas kernels for 0% -> 0%
where the time goes in v1:
time: 1110 us
  waiting for transfers between devices  982 us (88%)
  matrix products  68.1 us (6%)
  local copies, waits for them, and re-layouts  31.3 us (3%)
  other arithmetic  17.8 us (2%)
  between operations  14 us (1%)
    unnamed x5, waiting for transfers between devices  669 us
    reduce_scatter x1, waiting for transfers between devices, shards(): lax.psum_scatter(weight_term, ('rep', 'seq'), scatter_dimension=0, tiled=...  161 us
    all_gather x1, waiting for transfers between devices, shards(): shard_rows = lax.all_gather(kv_latent[0], 'seq', axis=0, tiled=True)  80.6 us
    all_gather x1, waiting for transfers between devices, shards(): lax.all_gather(query_term, axis_name='head')  71.6 us
  transfers between devices with their start and end apart: 4, of which 4 were waited for; matrix products, arithmetic and copies ran while one was open for 5% of the time, Pallas kernels for 0%

profile of v1, /device:TPU:2, one launch (start us, length us, event | category | flops | bytes accessed | tf_op | source)
XLA Modules:
  0.0 1113.7 jit_solution(3270590368468296238)
XLA Ops:
  7.2 1.8 copy.33
  10.2 6.6 copy.32
  16.8 3.7 convolution_bitcast_fusion.1
  22.0 80.6 %all-gather.5.cloned.1.call-done = bf16[1,2048,576]{2,1,0:T(8,128)(2,1)} async-done(((bf16[1,128,576]{2,1,0:T(8,128)(2,1)}), bf16[1,2048,576]{2,1,0:T(8,128)(2,1)}) %all-gather.5.cloned.1.call-update) | async-done | bytes 2359312 | tf_op jit(solution)/shard_map/all_gather | solution.py:65
  103.9 6.8 convert_bitcast_fusion
  111.2 4.8 fusion.12
  116.3 2.0 fusion.11
  118.3 5.7 fusion.47
  124.0 6.7 fusion.19
  130.8 15.9 %convolution_convert_fusion = bf16[8,2048,192]{1,2,0:T(8,128)(2,1)} fusion(f32[8,2048,128]{1,2,0:T(8,128)} %fusion.12, bf16[8,128,32]{1,2,0:T(8,128)(2,1)S(1)} %get-tuple-element.17, bf16[8,128,32]{1,2,0:T(8,128)(2,1)S(1)} %get-tuple-element.16, bf16[8,128,128]{1,2,0:T(8,128)(2,1)S(1)} %slice.89, f32[8,128,2048]{2,1,0:T(8,128)} %get-tuple-element.21, ...), kind=kOutput, calls=%fused_computation.19 | convolution fusion | flops 824314880 | bytes 23465984 | tf_op jit(solution)/shard_map/hqk,hqd->hkd/dot_general | solution.py:101
  146.7 2.1 convert_reduce_fusion
  150.2 1.2 copy-done.5
  151.4 4.5 fusion.23
  155.9 2.7 pad_maximum_fusion.3
  158.6 5.9 copy.49
  164.5 14.7 %fusion.10 = f32[8,128,192]{1,2,0:T(8,128)S(1)} fusion(bf16[8,2048,64]{1,2,0:T(8,128)(2,1)S(1)} %broadcast_in_dim.13, bf16[8,2048,128]{1,2,0:T(8,128)(2,1)} %copy-done.1, f32[8,2048,128]{1,2,0:T(8,128)} %fusion.12, f32[8,128,2048]{2,1,0:T(8,128)} %get-tuple-element.21, f32[8,128]{1,0:T(8,128)S(1)} %get-tuple-element.20), kind=kOutput, calls=%fused_computation.16 | convolution fusion | flops 832572416 | bytes 23859200 | tf_op jit(solution)/shard_map/hqk,hkd->hqd/dot_general | solution.py:98
  179.3 4.1 convolution_bitcast_fusion
  183.4 5.0 fusion.31
  188.4 9.7 copy.42
  198.1 669.2 %reduce-scatter.7.cloned.1.call-done = f32[16,576]{1,0:T(8,128)} async-done(((f32[2048,576]{1,0:T(8,128)}), f32[16,576]{1,0:T(8,128)}) %reduce-scatter.7.cloned.1.call-update) | async-done | bytes 36880
  869.0 71.6 %all-gather.7.cloned.1.call-done = f32[1024,1536]{1,0:T(8,128)} async-done(((f32[128,1536]{1,0:T(8,128)}), f32[1024,1536]{1,0:T(8,128)}) %all-gather.7.cloned.1.call-update) | async-done | bytes 6291472 | tf_op jit(solution)/shard_map/all_gather | solution.py:110
  940.6 4.1 reduce_sum.38
  944.7 160.8 %reduce-scatter.5.cloned.1.call-done = f32[48,1536]{1,0:T(8,128)} async-done(((f32[1536,1536]{1,0:T(8,128)}), f32[48,1536]{1,0:T(8,128)}) %reduce-scatter.5.cloned.1.call-update) | async-done | bytes 294928 | tf_op jit(solution)/shard_map/reduce_scatter | solution.py:128
  1105.5 1.6 convert_element_type.55
  (37 shorter events, 7.9 us)
Async XLA Ops:
  7.2 9.7 copy-start
  7.2 95.4 %all-gather.5.cloned.1.call-start = ((), (), s32[]{:S(2)}) async-start(), calls=%async_computation.3 | async-start | bytes 2785280 | tf_op jit(solution)/shard_map/all_gather | solution.py:65
  9.0 858.3 %reduce-scatter.7.cloned.1.call-start = ((), (), s32[]{:S(2)}) async-start(), calls=%async_computation.5 | async-start | bytes 5283840
  10.2 10.4 copy-start.3
  111.2 5.0 copy-start.1
  116.3 2.0 copy-start.2
  146.7 2.8 slice-start
  146.7 3.5 copy-start.4
  146.7 4.7 copy-start.5
  164.5 776.1 %all-gather.7.cloned.1.call-start = ((), (), s32[]{:S(2)}) async-start(), calls=%async_computation.4 | async-start | bytes 7077888 | tf_op jit(solution)/shard_map/all_gather | solution.py:110
  183.4 922.1 %reduce-scatter.5.cloned.1.call-start = ((), (), s32[]{:S(2)}) async-start(), calls=%async_computation.2 | async-start | bytes 9732096 | tf_op jit(solution)/shard_map/reduce_scatter | solution.py:128
Sparse Core Ops, SparseCore 0:
  10.6 92.0 all-gather.4
  164.6 702.6 reduce-scatter.6
  869.1 71.3 all-gather.6
  944.9 160.5 reduce-scatter.4
